TPU v7x, 256 devices: a whole 4x4x8 slice. The times are simulated.
256 devices in a mesh: mem: 16 (over y, x), tile: 16 (over z, core).
Axes of the slice: x: 4, y: 4, z: 8, core: 2. Of those that a mesh axis runs over, the one named last changes fastest.
Arguments:
- ensemble: float32 [1024, 3, 128, 256], P('mem', None, 'tile'), may hold values from -4.5 to 5
- obs_cells: int32 [16, 256], replicated, may hold values from 0 to 6143
- region_tile: int32 [16], replicated, may hold values from 0 to 15, each once
- obs_values: float32 [16, 256], replicated, may hold values from -5.6 to 5.6
- obs_error: float32 [16, 256], replicated, may hold values from 0.05 to 0.75
Outputs:
- analysis: float32 [1024, 3, 128, 256], P('mem', None, 'tile')
Inputs may be any that keep to these rules, and one draw needn't show every extreme that they name: `obs_cells`: row r lists flat indices into the values of tile region_tile[r], ordered by field, then row within the tile, then column; indices may repeat. `region_tile`: each tile holds exactly one region.
All inputs are finite; a program needn't handle non-finite values.
Results may differ from a plain program's by a relative error of at most 0.00029.
Values sent between devices are 32-bit elements; how exact they have to be, the bound alone decides.
A program may use at most 64 MiB of HBM per device.

v0:
```python
import functools
import math

import jax
import jax.numpy as jnp
from jax import lax
from jax.experimental import pallas as pl
from jax.experimental.pallas import tpu as pltpu
from jax.sharding import PartitionSpec as P

MEMBERS = 1024
STEPS = 4
DEGREE = 4
SIDE = 4
N_MEM = 16
N_TILE = 16
ROWS = 8
LONS = 256
LANES = 128
OBS = 256
OWN = MEMBERS // N_MEM
COLS = 3 * LANES
CHUNK = 16
CHUNKS = OWN // CHUNK
GROUP = SIDE * OWN

MESH = pl.DeviceIdType.MESH
F32, BF16 = jnp.float32, jnp.bfloat16

FAR_FIRST = (2, 1, 3, 0)
OFFSETS = [(dy, dx) for dy in FAR_FIRST for dx in FAR_FIRST if (dy, dx) != (0, 0)]


def dot(a, b):
    return jnp.dot(a, b, preferred_element_type=F32)


def split(a):
    high = a.astype(BF16)
    return high, (a - high.astype(F32)).astype(BF16)


def dot_split(ah, al, bh, bl):
    return dot(ah, bh) + (dot(ah, bl) + dot(al, bh))


def matmul(a, b):
    return dot_split(*split(a), *split(b))


def total(a):
    return jnp.sum(jnp.sum(a, axis=0, keepdims=True), axis=1, keepdims=True)


def advanced(load):
    h, u, v = load(0, 1), load(1, 1), load(2, 1)
    hs, us, vs = load(0, 0), load(1, 0), load(2, 0)
    hn, un, vn = load(0, 2), load(1, 2), load(2, 2)
    he, hw = pltpu.roll(h, LONS - 1, 1), pltpu.roll(h, 1, 1)
    ue, uw = pltpu.roll(u, LONS - 1, 1), pltpu.roll(u, 1, 1)
    ve, vw = pltpu.roll(v, LONS - 1, 1), pltpu.roll(v, 1, 1)
    flux = ((1.0 + he) * ue - (1.0 + hw) * uw) + ((1.0 + hn) * vn - (1.0 + hs) * vs)
    push_u = u * (ue - uw) + v * (un - us) + (he - hw) - v
    push_v = u * (ve - vw) + v * (vn - vs) + (hn - hs) + u
    return (
        0.6 * h + 0.1 * ((he + hw) + (hn + hs)) - 0.15 * flux,
        0.6 * u + 0.1 * ((ue + uw) + (un + us)) - 0.15 * push_u,
        0.6 * v + 0.1 * ((ve + vw) + (vn + vs)) - 0.15 * push_v,
    )


def spectral_map(norm):
    bound = 2.0 + norm
    values = []
    for j in range(DEGREE + 1):
        angle = (j + 0.5) * (math.pi / (DEGREE + 1))
        values.append(lax.rsqrt(0.5 * (bound + 1.0) + (0.5 * math.cos(angle)) * (bound - 1.0)))
    coeffs = []
    for k in range(DEGREE + 1):
        factor = 2.0 / (DEGREE + 1) * (0.5 if k == 0 else 1.0)
        terms = [
            (factor * math.cos(k * (j + 0.5) * (math.pi / (DEGREE + 1)))) * values[j]
            for j in range(DEGREE + 1)
        ]
        coeffs.append(sum(terms[1:], terms[0]))
    return 2.0 / (bound - 1.0), coeffs


def kernel(
    state, slab_ref, lane_ref, goal_ref, error_ref, out,
    wide, ping, pong, outgoing, seen, columns, observed, sums_out, sums_in,
    uth, utl, uh, ul, dh, dl, result,
    load_sem, halo_send, halo_recv, obs_send, obs_recv, col_send, col_recv,
    sum_send, sum_recv, back_send, back_recv,
):
    me = lax.axis_index("mem")
    tile = lax.axis_index("tile")
    mine_y, mine_x = me // SIDE, lax.rem(me, SIDE)
    above, below = lax.rem(tile + 1, N_TILE), lax.rem(tile + N_TILE - 1, N_TILE)

    def peer(dy, dx):
        return lax.rem(mine_y + dy, SIDE) * SIDE + lax.rem(mine_x + dx, SIDE)

    def members(c):
        return pl.ds(pl.multiple_of(c * CHUNK, CHUNK), CHUNK)

    def block(i):
        return pl.ds(pl.multiple_of(i * OWN, OWN), OWN)

    def load_copy(c):
        part = members(c)
        return pltpu.make_async_copy(
            state.at[:, :, part, :], wide.at[:, STEPS : STEPS + ROWS, part, :], load_sem.at[c]
        )

    def halo_copy(c, side):
        part = members(c)
        first, into, to = ((ROWS - STEPS, 0, above), (0, STEPS + ROWS, below))[side]
        return pltpu.make_async_remote_copy(
            src_ref=state.at[:, first : first + STEPS, part, :],
            dst_ref=wide.at[:, into : into + STEPS, part, :],
            send_sem=halo_send.at[side, c],
            recv_sem=halo_recv.at[side, c],
            device_id={"tile": to},
            device_id_type=MESH,
        )

    def obs_copy(c, n, to):
        return pltpu.make_async_remote_copy(
            src_ref=seen.at[members(c), :],
            dst_ref=observed.at[pl.ds(pl.multiple_of(me * OWN + c * CHUNK, CHUNK), CHUNK), :],
            send_sem=obs_send.at[n],
            recv_sem=obs_recv.at[me],
            device_id={"mem": to},
            device_id_type=MESH,
        )

    def col_copy(n, to):
        return pltpu.make_async_remote_copy(
            src_ref=outgoing.at[to],
            dst_ref=columns.at[block(me), :],
            send_sem=col_send.at[n],
            recv_sem=col_recv.at[me],
            device_id={"mem": to},
            device_id_type=MESH,
        )

    def sum_copy(n, to):
        return pltpu.make_async_remote_copy(
            src_ref=sums_out,
            dst_ref=sums_in.at[tile],
            send_sem=sum_send.at[n],
            recv_sem=sum_recv.at[tile],
            device_id={"tile": to},
            device_id_type=MESH,
        )

    def back_copy(n, to):
        return pltpu.make_async_remote_copy(
            src_ref=result.at[block(to), :],
            dst_ref=out.at[me],
            send_sem=back_send.at[n],
            recv_sem=back_recv.at[me],
            device_id={"mem": to},
            device_id_type=MESH,
        )

    def wait_for(ref, sem):
        pltpu.make_async_copy(ref, ref, sem).wait()

    for c in range(CHUNKS):
        load_copy(c).start()
    barrier = pltpu.get_barrier_semaphore()
    for dy, dx in OFFSETS:
        pl.semaphore_signal(barrier, inc=1, device_id={"mem": peer(dy, dx)}, device_id_type=MESH)
    for k in range(1, N_TILE):
        to = lax.rem(tile + k, N_TILE)
        pl.semaphore_signal(barrier, inc=1, device_id={"tile": to}, device_id_type=MESH)
    pl.semaphore_wait(barrier, N_MEM + N_TILE - 2)
    for c in range(CHUNKS):
        halo_copy(c, 0).start()
        halo_copy(c, 1).start()

    def forecast(c, carry):
        part = members(c)
        load_copy(c).wait()
        wait_for(wide.at[:, 0:STEPS, part, :], halo_recv.at[0, c])
        wait_for(wide.at[:, 0:STEPS, part, :], halo_recv.at[1, c])

        def step(count, read, write):
            def row(i, carry):
                new = advanced(lambda f, k: read(f, i + k))
                for f in range(3):
                    write[f, i] = new[f]
                return carry

            lax.fori_loop(0, count, row, 0)

        step(ROWS + 6, lambda f, i: wide[f, i, part, :], ping)
        step(ROWS + 4, lambda f, i: ping[f, i], pong)
        step(ROWS + 2, lambda f, i: pong[f, i], ping)

        def last(i, found):
            new = advanced(lambda f, k: ping[f, i + k])
            found = list(found)
            for f in range(3):
                for half in range(2):
                    values = new[f][:, half * LANES : (half + 1) * LANES]
                    outgoing[2 * i + half, part, f * LANES : (f + 1) * LANES] = values
                    slab = f * (2 * ROWS) + 2 * i + half
                    for g in range(2):
                        lanes = slice(g * LANES, (g + 1) * LANES)
                        here = slab_ref[:, lanes] == slab
                        for s in range(CHUNK // 8):
                            n = g * (CHUNK // 8) + s
                            taken = jnp.take_along_axis(
                                values[s * 8 : s * 8 + 8], lane_ref[:, lanes], axis=1
                            )
                            found[n] = jnp.where(here, taken, found[n])
            return tuple(found)

        none = jnp.zeros((8, LANES), F32)
        found = lax.fori_loop(0, ROWS, last, (none,) * (2 * (CHUNK // 8)))
        for g in range(2):
            for s in range(CHUNK // 8):
                at = pl.multiple_of(c * CHUNK + s * 8, 8)
                seen[pl.ds(at, 8), g * LANES : (g + 1) * LANES] = found[g * (CHUNK // 8) + s]
        for n, (dy, dx) in enumerate(OFFSETS):
            obs_copy(c, n, peer(dy, dx)).start()
        return carry

    lax.fori_loop(0, CHUNKS, forecast, 0)
    for n, (dy, dx) in enumerate(OFFSETS):
        col_copy(n, peer(dy, dx)).start()
    observed[block(me), :] = seen[...]
    columns[block(me), :] = outgoing[me]

    for dy, dx in OFFSETS:
        src = peer(dy, dx)
        wait_for(observed.at[block(src), :], obs_recv.at[src])
    obs_mean = jnp.sum(observed[...], axis=0, keepdims=True) * (1.0 / MEMBERS)
    error = error_ref[...]
    weight = lax.rsqrt(error)
    misfit = goal_ref[...] - obs_mean
    square = jnp.zeros((1, OBS), F32)
    for b in range(MEMBERS // LANES):
        rows = slice(b * LANES, (b + 1) * LANES)
        centred = observed[rows, :] - obs_mean
        square = square + jnp.sum(centred * centred, axis=0, keepdims=True)
        scaled = centred * weight
        uh[rows, :], ul[rows, :] = split(scaled)
        uth[:, rows], utl[:, rows] = split(scaled.T)
    misfit_sum = total(misfit * misfit)
    spread_sum = total(square * (1.0 / (MEMBERS - 1)) + error)
    upper = lax.broadcasted_iota(jnp.int32, (8, LANES), 0) < 4
    sums_out[...] = jnp.where(upper, misfit_sum, spread_sum)
    for k in range(1, N_TILE):
        sum_copy(k, lax.rem(tile + k, N_TILE)).start()
    sums_in[tile] = sums_out[...]
    inner = dot_split(uth[...], utl[...], uh[...], ul[...])
    norm = jnp.sqrt(total(inner * inner))
    for k in range(1, N_TILE):
        src = lax.rem(tile + k, N_TILE)
        wait_for(sums_in.at[src], sum_recv.at[src])
    sums = jnp.sum(sums_in[...], axis=0)
    inflation = sums[0:1, 0:1] / sums[4:5, 0:1]

    gain = inflation * (1.0 / (MEMBERS - 1))
    root = jnp.sqrt(inflation)
    scale, c = spectral_map(gain * norm)
    p0 = c[0] - c[1] + c[2] - c[3] + c[4]
    eye = (
        lax.broadcasted_iota(jnp.int32, (OBS, OBS), 0)
        == lax.broadcasted_iota(jnp.int32, (OBS, OBS), 1)
    ).astype(F32)
    lifted = (scale * gain) * inner
    a = lifted - eye
    a2 = matmul(a, a)
    a3 = matmul(a2, a)
    r = (
        c[1] * eye
        + (2.0 * c[2]) * (a - eye)
        + c[3] * (4.0 * (a2 - a) + eye)
        + (8.0 * c[4]) * (a3 - a2)
    )
    lifted_split = split(lifted)
    r_split = split(r)
    h = jnp.broadcast_to(misfit * weight, (8, OBS))
    for _ in range(2):
        h = p0 * h + dot_split(*split(dot_split(*split(h), *r_split)), *lifted_split)
    h_split = split(gain * h)

    for dy, dx in OFFSETS:
        src = peer(dy, dx)
        wait_for(columns.at[block(src), :], col_recv.at[src])
    centre = jnp.sum(columns[...], axis=0, keepdims=True) * (1.0 / MEMBERS)
    for b in range(MEMBERS // LANES):
        rows = slice(b * LANES, (b + 1) * LANES)
        dh[rows, :], dl[rows, :] = split(columns[rows, :] - centre)
    cross_split = split(dot_split(uth[...], utl[...], dh[...], dl[...]))
    moved_split = split((root * scale * gain) * dot_split(*r_split, *cross_split))
    base = centre + dot_split(*h_split, *cross_split)[0:1, :]
    keep = root * p0
    order = {offset: n for n, offset in enumerate(OFFSETS)}
    for dy in FAR_FIRST:
        q = lax.rem(mine_y + dy, SIDE)
        rows = pl.ds(pl.multiple_of(q * GROUP, GROUP), GROUP)
        shift = dot_split(uh[rows, :], ul[rows, :], *moved_split)
        result[rows, :] = base + (keep * (columns[rows, :] - centre) + shift)
        for dx in FAR_FIRST:
            if (dy, dx) in order:
                back_copy(order[dy, dx], peer(dy, dx)).start()
    out[me] = result[block(me), :]

    for n, (dy, dx) in enumerate(OFFSETS):
        src = peer(dy, dx)
        wait_for(out.at[src], back_recv.at[src])
    for c in range(CHUNKS):
        halo_copy(c, 0).wait_send()
        halo_copy(c, 1).wait_send()
    for n, (dy, dx) in enumerate(OFFSETS):
        to = peer(dy, dx)
        wait_for(seen, obs_send.at[n])
        col_copy(n, to).wait_send()
        back_copy(n, to).wait_send()
    for k in range(1, N_TILE):
        sum_copy(k, lax.rem(tile + k, N_TILE)).wait_send()


def on_device(ensemble, obs_cells, region_tile, obs_values, obs_error):
    chosen = (region_tile == lax.axis_index("tile"))[:, None]
    cells = jnp.sum(jnp.where(chosen, obs_cells, 0), axis=0)
    goal = jnp.sum(jnp.where(chosen, obs_values, 0.0), axis=0)[None, :]
    error = jnp.sum(jnp.where(chosen, obs_error, 0.0), axis=0)[None, :]
    slab = jnp.broadcast_to(cells // LANES, (8, OBS))
    lane = jnp.broadcast_to(cells % LANES, (8, OBS))
    state = jnp.transpose(ensemble, (1, 2, 0, 3))
    vmem = pl.BlockSpec(memory_space=pltpu.VMEM)
    dma = pltpu.SemaphoreType.DMA
    updated = pl.pallas_call(
        kernel,
        name="analysis",
        out_shape=jax.ShapeDtypeStruct((N_MEM, OWN, COLS), F32),
        in_specs=[pl.BlockSpec(memory_space=pl.ANY), vmem, vmem, vmem, vmem],
        out_specs=vmem,
        scratch_shapes=[
            pltpu.VMEM((3, ROWS + 2 * STEPS, OWN, LONS), F32),
            pltpu.VMEM((3, ROWS + 6, CHUNK, LONS), F32),
            pltpu.VMEM((3, ROWS + 4, CHUNK, LONS), F32),
            pltpu.VMEM((N_MEM, OWN, COLS), F32),
            pltpu.VMEM((OWN, OBS), F32),
            pltpu.VMEM((MEMBERS, COLS), F32),
            pltpu.VMEM((MEMBERS, OBS), F32),
            pltpu.VMEM((8, LANES), F32),
            pltpu.VMEM((N_TILE, 8, LANES), F32),
            pltpu.VMEM((OBS, MEMBERS), BF16),
            pltpu.VMEM((OBS, MEMBERS), BF16),
            pltpu.VMEM((MEMBERS, OBS), BF16),
            pltpu.VMEM((MEMBERS, OBS), BF16),
            pltpu.VMEM((MEMBERS, COLS), BF16),
            pltpu.VMEM((MEMBERS, COLS), BF16),
            pltpu.VMEM((MEMBERS, COLS), F32),
            dma((CHUNKS,)),
            dma((2, CHUNKS)),
            dma((2, CHUNKS)),
            dma((N_MEM,)),
            dma((N_MEM,)),
            dma((N_MEM,)),
            dma((N_MEM,)),
            dma((N_TILE,)),
            dma((N_TILE,)),
            dma((N_MEM,)),
            dma((N_MEM,)),
        ],
        compiler_params=pltpu.CompilerParams(
            collective_id=0, has_side_effects=True, vmem_limit_bytes=44 << 20
        ),
    )(state, slab, lane, goal, error)
    updated = updated.reshape(ROWS, 2, OWN, 3, LANES)
    return jnp.transpose(updated, (2, 3, 0, 1, 4)).reshape(ensemble.shape)


def solution(mesh):
    in_specs = (P("mem", None, "tile", None), P(), P(), P(), P())
    out_specs = P("mem", None, "tile", None)
    return jax.shard_map(
        on_device, mesh=mesh, in_specs=in_specs, out_specs=out_specs, check_vma=False
    )
```

profile of v0, /device:TPU:1, one launch (start us, length us, event | category | flops | bytes accessed | tf_op | source)
XLA Modules:
  0.0 101.9 jit_solution(1931337332496194582)
XLA Ops:
  0.0 0.7 broadcast_compare_fusion.2
  0.7 0.8 select_reduce_fusion.2
  1.5 0.8 select_reduce_fusion
  2.3 1.9 %copy.14 = f32[64,3,8,256]{3,0,2,1:T(8,128)S(1)} copy(f32[64,3,8,256]{3,2,1,0:T(8,128)} %param.5) | data formatting | bytes 3145728 | tf_op args[0]
  4.2 92.3 %analysis.1 = f32[16,64,384]{2,1,0:T(8,128)S(1)} custom-call(f32[3,8,64,256]{3,2,1,0:T(8,128)S(1)} %bitcast.9, s32[8,256]{1,0:T(8,128)S(1)} %broadcast_in_dim.41.slab_ref, s32[8,256]{1,0:T(8,128)S(1)} %broadcast_in_dim.42.lane_ref, f32[1,256]{1,0:T(1,128)S(1)} %bitcast.11, f32[1,256]{1,0:T(1,128)S(1)} %bitcast.10), custom_call_target="tpu_custom_call" | custom-call | tf_op jit(solution)/shard_map/analysis/pallas_call | solution.py:340
  96.5 1.7 %reshape.7 = f32[8,2,64,3,128]{4,3,2,1,0:T(4,128)} reshape(f32[16,64,384]{2,1,0:T(8,128)S(1)} %analysis.1) | data formatting | bytes 3145728 | tf_op jit(solution)/shard_map/reshape | solution.py:379
  98.2 3.6 %copy.13 = f32[64,3,8,2,128]{4,2,3,1,0:T(8,128)} copy(f32[64,3,8,2,128]{4,1,0,3,2:T(4,128)} %bitcast.12) | data formatting | bytes 3145728 | tf_op jit(solution)/shard_map/transpose | solution.py:380
  (3 shorter events, 0.0 us)
where the time goes:
time: 102 us
  Pallas kernels  92.3 us (90%)
  local copies, waits for them, and re-layouts  7.27 us (7%)
  other arithmetic  2.3 us (2%)
    pallas_call x1, Pallas kernels, on_device(): pl.pallas_call(kernel, name='analysis', out_shape=jax.ShapeDtypeStruct((N...  92.3 us
    transpose x1, local copies, waits for them, and re-layouts, on_device(): return jnp.transpose(updated, (2, 3, 0, 1, 4)).reshape(ensemble.shape)  3.65 us

commit v1 on v0

v1 whole, which is shorter than its diff:
```python
import functools
import math

import jax
import jax.numpy as jnp
from jax import lax
from jax.experimental import pallas as pl
from jax.experimental.pallas import tpu as pltpu
from jax.sharding import PartitionSpec as P

MEMBERS = 1024
STEPS = 4
DEGREE = 4
SIDE = 4
N_MEM = 16
N_TILE = 16
ROWS = 8
LONS = 256
LANES = 128
OBS = 256
OWN = MEMBERS // N_MEM
LINES = 3 * ROWS
COLS = 3 * LANES
CHUNK = 8
CHUNKS = OWN // CHUNK
GROUP = SIDE * OWN

MESH = pl.DeviceIdType.MESH
F32, BF16 = jnp.float32, jnp.bfloat16

PARTNERS = [(dy, (dy + k) % SIDE) for k in (2, 1, 3, 0) for dy in (2, 1, 3, 0)]
BACK = [PARTNERS.index((-dy % SIDE, -dx % SIDE)) for dy, dx in PARTNERS]
OTHERS = range(N_MEM - 1)
SELF = N_MEM - 1
ARRIVAL = (0, 2, 1, 3)
EARLY = 2


def dot(a, b):
    return jnp.dot(a, b, preferred_element_type=F32)


def split(a):
    high = a.astype(BF16)
    return high, (a - high.astype(F32)).astype(BF16)


def dot_split(ah, al, bh, bl):
    return dot(ah, bh) + (dot(ah, bl) + dot(al, bh))


def matmul(a, b):
    return dot_split(*split(a), *split(b))


def total(a):
    return jnp.sum(jnp.sum(a, axis=0, keepdims=True), axis=1, keepdims=True)


def advanced(load):
    h, u, v = load(0, 1), load(1, 1), load(2, 1)
    hs, us, vs = load(0, 0), load(1, 0), load(2, 0)
    hn, un, vn = load(0, 2), load(1, 2), load(2, 2)
    he, hw = pltpu.roll(h, LONS - 1, 1), pltpu.roll(h, 1, 1)
    ue, uw = pltpu.roll(u, LONS - 1, 1), pltpu.roll(u, 1, 1)
    ve, vw = pltpu.roll(v, LONS - 1, 1), pltpu.roll(v, 1, 1)
    flux = ((1.0 + he) * ue - (1.0 + hw) * uw) + ((1.0 + hn) * vn - (1.0 + hs) * vs)
    push_u = u * (ue - uw) + v * (un - us) + (he - hw) - v
    push_v = u * (ve - vw) + v * (vn - vs) + (hn - hs) + u
    return (
        0.6 * h + 0.1 * ((he + hw) + (hn + hs)) - 0.15 * flux,
        0.6 * u + 0.1 * ((ue + uw) + (un + us)) - 0.15 * push_u,
        0.6 * v + 0.1 * ((ve + vw) + (vn + vs)) - 0.15 * push_v,
    )


def spectral_map(norm):
    bound = 2.0 + norm
    values = []
    for j in range(DEGREE + 1):
        angle = (j + 0.5) * (math.pi / (DEGREE + 1))
        values.append(lax.rsqrt(0.5 * (bound + 1.0) + (0.5 * math.cos(angle)) * (bound - 1.0)))
    coeffs = []
    for k in range(DEGREE + 1):
        factor = 2.0 / (DEGREE + 1) * (0.5 if k == 0 else 1.0)
        terms = [
            (factor * math.cos(k * (j + 0.5) * (math.pi / (DEGREE + 1)))) * values[j]
            for j in range(DEGREE + 1)
        ]
        coeffs.append(sum(terms[1:], terms[0]))
    return 2.0 / (bound - 1.0), coeffs


def kernel(
    state, cells_in, region_in, goals_in, errors_in, out,
    cells_ref, region_ref, goals_ref, errors_ref, raw, wide, ping, pong, slab_ref, lane_ref, outgoing, seen, columns, observed, sums_out, sums_in,
    uth, utl, uh, ul, cross, result, returned, ready,
    small_sem, load_sem, halo_send, halo_recv, obs_send, obs_recv, col_send, col_recv,
    sum_send, sum_recv, back_send, back_recv, out_sem,
):
    me = lax.axis_index("mem")
    tile = lax.axis_index("tile")
    mine_y, mine_x = me // SIDE, lax.rem(me, SIDE)
    above, below = lax.rem(tile + 1, N_TILE), lax.rem(tile + N_TILE - 1, N_TILE)

    def peer(n):
        dy, dx = PARTNERS[n]
        return lax.rem(mine_y + dy, SIDE) * SIDE + lax.rem(mine_x + dx, SIDE)

    def members(c):
        return pl.ds(pl.multiple_of(c * CHUNK, CHUNK), CHUNK)

    def block(n):
        return slice(n * OWN, (n + 1) * OWN)

    def load_copy(c):
        part = pl.ds(c * CHUNK * LINES, CHUNK * LINES)
        return [
            pltpu.make_async_copy(
                state.at[part, half * LANES : (half + 1) * LANES],
                raw.at[half, part, :],
                load_sem.at[c, half],
            )
            for half in range(2)
        ]

    def halo_copy(c, side):
        part = members(c)
        first, into, to = ((ROWS, 0, above), (STEPS, STEPS + ROWS, below))[side]
        return pltpu.make_async_remote_copy(
            src_ref=wide.at[:, first : first + STEPS, part, :],
            dst_ref=wide.at[:, into : into + STEPS, part, :],
            send_sem=halo_send.at[side, c],
            recv_sem=halo_recv.at[side, c],
            device_id={"tile": to},
            device_id_type=MESH,
        )

    def obs_copy(n, c, chunks):
        count = chunks * CHUNK
        first = pl.multiple_of(c * CHUNK, CHUNK)
        return pltpu.make_async_remote_copy(
            src_ref=seen.at[pl.ds(first, count), :],
            dst_ref=observed.at[pl.ds(BACK[n] * OWN + first, count), :],
            send_sem=obs_send.at[n],
            recv_sem=obs_recv.at[BACK[n]],
            device_id={"mem": peer(n)},
            device_id_type=MESH,
        )

    def col_copy(n, c, chunks):
        count = chunks * CHUNK
        first = pl.multiple_of(c * CHUNK, CHUNK)
        return pltpu.make_async_remote_copy(
            src_ref=outgoing.at[peer(n), pl.ds(first, count), :],
            dst_ref=columns.at[pl.ds(BACK[n] * OWN + first, count), :],
            send_sem=col_send.at[n],
            recv_sem=col_recv.at[BACK[n]],
            device_id={"mem": peer(n)},
            device_id_type=MESH,
        )

    def sum_copy(n, to):
        return pltpu.make_async_remote_copy(
            src_ref=sums_out,
            dst_ref=sums_in.at[tile],
            send_sem=sum_send.at[n],
            recv_sem=sum_recv.at[tile],
            device_id={"tile": to},
            device_id_type=MESH,
        )

    def back_copy(n):
        return pltpu.make_async_remote_copy(
            src_ref=result.at[block(n), :],
            dst_ref=returned.at[me],
            send_sem=back_send.at[n],
            recv_sem=back_recv.at[me],
            device_id={"mem": peer(n)},
            device_id_type=MESH,
        )

    def wait_for(ref, sem):
        pltpu.make_async_copy(ref, ref, sem).wait()

    small = [
        pltpu.make_async_copy(src, dst, small_sem.at[n])
        for n, (src, dst) in enumerate(
            [
                (region_in, region_ref),
                (cells_in, cells_ref),
                (goals_in, goals_ref),
                (errors_in, errors_ref),
            ]
        )
    ]
    for c in range(CHUNKS):
        for copy in load_copy(c):
            copy.start()
    for copy in small:
        copy.start()
    barrier = pltpu.get_barrier_semaphore()
    for n in OTHERS:
        pl.semaphore_signal(barrier, inc=1, device_id={"mem": peer(n)}, device_id_type=MESH)
    for k in range(1, N_TILE):
        to = lax.rem(tile + k, N_TILE)
        pl.semaphore_signal(barrier, inc=1, device_id={"tile": to}, device_id_type=MESH)

    for copy in small:
        copy.wait()
    cells = jnp.zeros((1, OBS), jnp.int32)
    goal = jnp.zeros((1, OBS), F32)
    error = jnp.zeros((1, OBS), F32)
    for region in range(N_TILE):
        chosen = region_ref[region] == tile
        cells = jnp.where(chosen, cells_ref[region : region + 1, :], cells)
        goal = jnp.where(chosen, goals_ref[region : region + 1, :], goal)
        error = jnp.where(chosen, errors_ref[region : region + 1, :], error)
    cells = jnp.broadcast_to(cells, (8, OBS))
    slab_ref[...] = lax.shift_right_logical(cells, 7)
    lane_ref[...] = lax.bitwise_and(cells, LANES - 1)
    for c in range(CHUNKS):
        for copy in load_copy(c):
            copy.wait()
        for m in range(c * CHUNK, (c + 1) * CHUNK, 8):
            for f in range(3):
                for i in range(ROWS):
                    first = m * LINES + f * ROWS + i
                    for half in range(2):
                        lanes = slice(half * LANES, (half + 1) * LANES)
                        wide[f, STEPS + i, m : m + 8, lanes] = raw[
                            half, pl.ds(first, 8, stride=LINES), :
                        ]
    pl.semaphore_wait(barrier, N_MEM + N_TILE - 2)
    for c in range(CHUNKS):
        halo_copy(c, 0).start()
        halo_copy(c, 1).start()

    def forecast(c, carry):
        part = members(c)
        wait_for(wide.at[:, 0:STEPS, part, :], halo_recv.at[0, c])
        wait_for(wide.at[:, 0:STEPS, part, :], halo_recv.at[1, c])

        def step(count, read, write):
            for i in range(count):
                new = advanced(lambda f, k: read(f, i + k))
                for f in range(3):
                    write[f, i] = new[f]

        step(ROWS + 6, lambda f, i: wide[f, i, part, :], ping)
        step(ROWS + 4, lambda f, i: ping[f, i], pong)
        step(ROWS + 2, lambda f, i: pong[f, i], ping)

        found = [jnp.zeros((8, LANES), F32)] * (2 * (CHUNK // 8))
        for i in range(ROWS):
            new = advanced(lambda f, k: ping[f, i + k])
            for f in range(3):
                for half in range(2):
                    values = new[f][:, half * LANES : (half + 1) * LANES]
                    outgoing[2 * i + half, part, f * LANES : (f + 1) * LANES] = values
                    slab = f * (2 * ROWS) + 2 * i + half
                    for g in range(2):
                        lanes = slice(g * LANES, (g + 1) * LANES)
                        here = slab_ref[:, lanes] == slab
                        for s in range(CHUNK // 8):
                            n = g * (CHUNK // 8) + s
                            taken = jnp.take_along_axis(
                                values[s * 8 : s * 8 + 8],
                                lane_ref[:, lanes],
                                axis=1,
                                mode="promise_in_bounds",
                            )
                            found[n] = jnp.where(here, taken, found[n])
        for g in range(2):
            for s in range(CHUNK // 8):
                at = pl.multiple_of(c * CHUNK + s * 8, 8)
                seen[pl.ds(at, 8), g * LANES : (g + 1) * LANES] = found[g * (CHUNK // 8) + s]

        @pl.when(lax.rem(c, 2) == 1)
        def _():
            for n in OTHERS:
                obs_copy(n, c - 1, 2).start()

        @pl.when(c < EARLY)
        def _():
            for n in OTHERS:
                col_copy(n, c, 1).start()

        return carry

    lax.fori_loop(0, CHUNKS, forecast, 0)
    for n in OTHERS:
        col_copy(n, EARLY, CHUNKS - EARLY).start()
    observed[block(SELF), :] = seen[...]
    columns[block(SELF), :] = outgoing[me]
    near = jnp.sum(outgoing[me], axis=0, keepdims=True) * (1.0 / OWN)

    for n in OTHERS:
        wait_for(observed.at[block(n), :], obs_recv.at[n])
    obs_mean = jnp.sum(observed[...], axis=0, keepdims=True) * (1.0 / MEMBERS)
    weight = lax.rsqrt(error)
    misfit = goal - obs_mean
    square = jnp.zeros((1, OBS), F32)
    for b in range(SIDE):
        rows = slice(b * GROUP, (b + 1) * GROUP)
        centred = observed[rows, :] - obs_mean
        square = square + jnp.sum(centred * centred, axis=0, keepdims=True)
        scaled = centred * weight
        uh[rows, :], ul[rows, :] = split(scaled)
        uth[b], utl[b] = split(scaled.T)
    misfit_sum = total(misfit * misfit)
    spread_sum = total(square * (1.0 / (MEMBERS - 1)) + error)
    upper = lax.broadcasted_iota(jnp.int32, (8, LANES), 0) < 4
    sums_out[...] = jnp.where(upper, misfit_sum, spread_sum)
    for k in range(1, N_TILE):
        sum_copy(k, lax.rem(tile + k, N_TILE)).start()
    sums_in[tile] = sums_out[...]
    inner = jnp.zeros((OBS, OBS), F32)
    for b in range(SIDE):
        rows = slice(b * GROUP, (b + 1) * GROUP)
        inner = inner + dot_split(uth[b], utl[b], uh[rows, :], ul[rows, :])
    norm = jnp.sqrt(total(inner * inner))
    for k in range(1, N_TILE):
        src = lax.rem(tile + k, N_TILE)
        wait_for(sums_in.at[src], sum_recv.at[src])
    sums = jnp.sum(sums_in[...], axis=0)
    inflation = sums[0:1, 0:1] / sums[4:5, 0:1]

    gain = inflation * (1.0 / (MEMBERS - 1))
    root = jnp.sqrt(inflation)
    scale, c = spectral_map(gain * norm)
    p0 = c[0] - c[1] + c[2] - c[3] + c[4]
    eye = (
        lax.broadcasted_iota(jnp.int32, (OBS, OBS), 0)
        == lax.broadcasted_iota(jnp.int32, (OBS, OBS), 1)
    ).astype(F32)
    lifted = (scale * gain) * inner
    a = lifted - eye
    a2 = matmul(a, a)
    a3 = matmul(a2, a)
    r = (
        c[1] * eye
        + (2.0 * c[2]) * (a - eye)
        + c[3] * (4.0 * (a2 - a) + eye)
        + (8.0 * c[4]) * (a3 - a2)
    )
    lifted_split = split(lifted)
    r_split = split(r)
    h = jnp.broadcast_to(misfit * weight, (8, OBS))
    for _ in range(2):
        h = p0 * h + dot_split(*split(dot_split(*split(h), *r_split)), *lifted_split)
    h_split = split(gain * h)

    column_sum = jnp.zeros((1, COLS), F32)
    for g in ARRIVAL:
        for n in range(g * SIDE, (g + 1) * SIDE):
            if n != SELF:
                wait_for(columns.at[block(n), :], col_recv.at[n])
        group = columns[g * GROUP : (g + 1) * GROUP, :]
        column_sum = column_sum + jnp.sum(group, axis=0, keepdims=True)
        part = dot_split(uth[g], utl[g], *split(group - near))
        cross[...] = part if g == ARRIVAL[0] else cross[...] + part
    centre = column_sum * (1.0 / MEMBERS)
    cross_split = split(cross[...])
    moved_split = split((root * scale * gain) * dot_split(*r_split, *cross_split))
    base = centre + dot_split(*h_split, *cross_split)[0:1, :]
    keep = root * p0
    for g in range(SIDE):
        rows = slice(g * GROUP, (g + 1) * GROUP)
        shift = dot_split(uh[rows, :], ul[rows, :], *moved_split)
        result[rows, :] = base + (keep * (columns[rows, :] - centre) + shift)
        for n in range(g * SIDE, (g + 1) * SIDE):
            if n != SELF:
                back_copy(n).start()
    returned[me] = result[block(SELF), :]

    finals = []
    for half in range(2):
        for i in range(ROWS):
            src = 2 * i + half

            @pl.when(src != me)
            def _():
                wait_for(returned.at[src], back_recv.at[src])

            for m in range(0, OWN, 8):
                for f in range(3):
                    ready[half, pl.ds(m * LINES + f * ROWS + i, 8, stride=LINES), :] = returned[
                        src, m : m + 8, f * LANES : (f + 1) * LANES
                    ]
        finals.append(
            pltpu.make_async_copy(
                ready.at[half], out.at[:, half * LANES : (half + 1) * LANES], out_sem.at[half]
            )
        )
        finals[-1].start()
    for c in range(CHUNKS):
        halo_copy(c, 0).wait_send()
        halo_copy(c, 1).wait_send()
    for n in OTHERS:
        wait_for(seen, obs_send.at[n])
        wait_for(outgoing.at[0], col_send.at[n])
        back_copy(n).wait_send()
    for k in range(1, N_TILE):
        sum_copy(k, lax.rem(tile + k, N_TILE)).wait_send()
    for copy in finals:
        copy.wait()


def on_device(ensemble, obs_cells, region_tile, obs_values, obs_error):
    state = ensemble.reshape(OWN * LINES, LONS)
    dma = pltpu.SemaphoreType.DMA
    updated = pl.pallas_call(
        kernel,
        name="analysis",
        out_shape=jax.ShapeDtypeStruct((OWN * LINES, LONS), F32),
        in_specs=[pl.BlockSpec(memory_space=pltpu.HBM)] * 5,
        out_specs=pl.BlockSpec(memory_space=pltpu.HBM),
        scratch_shapes=[
            pltpu.VMEM((N_TILE, OBS), jnp.int32),
            pltpu.SMEM((N_TILE,), jnp.int32),
            pltpu.VMEM((N_TILE, OBS), F32),
            pltpu.VMEM((N_TILE, OBS), F32),
            pltpu.VMEM((2, OWN * LINES, LANES), F32),
            pltpu.VMEM((3, ROWS + 2 * STEPS, OWN, LONS), F32),
            pltpu.VMEM((3, ROWS + 6, CHUNK, LONS), F32),
            pltpu.VMEM((3, ROWS + 4, CHUNK, LONS), F32),
            pltpu.VMEM((8, OBS), jnp.int32),
            pltpu.VMEM((8, OBS), jnp.int32),
            pltpu.VMEM((N_MEM, OWN, COLS), F32),
            pltpu.VMEM((OWN, OBS), F32),
            pltpu.VMEM((MEMBERS, COLS), F32),
            pltpu.VMEM((MEMBERS, OBS), F32),
            pltpu.VMEM((8, LANES), F32),
            pltpu.VMEM((N_TILE, 8, LANES), F32),
            pltpu.VMEM((SIDE, OBS, GROUP), BF16),
            pltpu.VMEM((SIDE, OBS, GROUP), BF16),
            pltpu.VMEM((MEMBERS, OBS), BF16),
            pltpu.VMEM((MEMBERS, OBS), BF16),
            pltpu.VMEM((OBS, COLS), F32),
            pltpu.VMEM((MEMBERS, COLS), F32),
            pltpu.VMEM((N_MEM, OWN, COLS), F32),
            pltpu.VMEM((2, OWN * LINES, LANES), F32),
            dma((4,)),
            dma((CHUNKS, 2)),
            dma((2, CHUNKS)),
            dma((2, CHUNKS)),
            dma((N_MEM,)),
            dma((N_MEM,)),
            dma((N_MEM,)),
            dma((N_MEM,)),
            dma((N_TILE,)),
            dma((N_TILE,)),
            dma((N_MEM,)),
            dma((N_MEM,)),
            dma((2,)),
        ],
        compiler_params=pltpu.CompilerParams(
            collective_id=0, has_side_effects=True, vmem_limit_bytes=60_000_000
        ),
    )(state, obs_cells, region_tile, obs_values, obs_error)
    return updated.reshape(ensemble.shape)


def solution(mesh):
    in_specs = (P("mem", None, "tile", None), P(), P(), P(), P())
    out_specs = P("mem", None, "tile", None)
    return jax.shard_map(
        on_device, mesh=mesh, in_specs=in_specs, out_specs=out_specs, check_vma=False
    )
```

time: 102 us -> 73.6 us (0.72)
  Pallas kernels: 92.3 us -> 70.8 us
  local copies, waits for them, and re-layouts: 7.27 us -> 2.65 us
  other arithmetic: 2.3 us -> 0 us
    pallas_call x1, Pallas kernels: 92.3 us -> 70.8 us  [on_device(): pl.pallas_call(kernel, name='analysis', out_shape=jax.ShapeDtypeStruct((O...]
    transpose x1 -> x0, local copies, waits for them, and re-layouts: 3.65 us -> none  [on_device(): return jnp.transpose(updated, (2, 3, 0, 1, 4)).reshape(ensemble.shape)]
    reshape x1 -> x0, local copies, waits for them, and re-layouts: 1.7 us -> none  [on_device(): updated = updated.reshape(ROWS, 2, OWN, 3, LANES)]
    reduce_sum x2 -> x0, other arithmetic: 1.63 us -> none  [the longest x1 0.82 us: on_device(): error = jnp.sum(jnp.where(chosen, obs_error, 0.0), axis=0)[None, :]]
where the time goes in v1:
time: 73.6 us; the launch traced here: 73.4 us
  Pallas kernels  70.8 us (96%)
  local copies, waits for them, and re-layouts  2.65 us (4%)
    pallas_call x1, Pallas kernels, on_device(): pl.pallas_call(kernel, name='analysis', out_shape=jax.ShapeDtypeStruct((O...  70.8 us
    unnamed x1, local copies, waits for them, and re-layouts  2.65 us

profile of v1, /device:TPU:1, one launch (start us, length us, event | category | flops | bytes accessed | tf_op | source)
XLA Modules:
  0.0 73.4 jit_solution(11075754554869150959)
XLA Ops:
  0.0 70.8 %analysis.1 = f32[1536,256]{1,0:T(8,128)} custom-call(f32[1536,256]{1,0:T(8,128)} %bitcast.3, s32[16,256]{1,0:T(8,128)} %cells_in.1, s32[16]{0:T(128)} %region_in.1, f32[16,256]{1,0:T(8,128)} %goals_in.1, f32[16,256]{1,0:T(8,128)} %errors_in.1), custom_call_target="tpu_custom_call" | custom-call | tf_op jit(solution)/shard_map/analysis/pallas_call | solution.py:413
  70.8 2.7 %copy.7 = f32[64,3,8,256]{3,2,1,0:T(8,128)} copy(f32[64,3,8,256]{3,2,1,0:T(8,128)} %bitcast.2) | data formatting | bytes 3145728

commit v2 on v1

--- a/solution.py
+++ b/solution.py
@@ -20,7 +20,6 @@
 OBS = 256
 OWN = MEMBERS // N_MEM
 LINES = 3 * ROWS
-COLS = 3 * LANES
 CHUNK = 8
 CHUNKS = OWN // CHUNK
 GROUP = SIDE * OWN
@@ -94,8 +93,8 @@
 def kernel(
     state, cells_in, region_in, goals_in, errors_in, out,
     cells_ref, region_ref, goals_ref, errors_ref, raw, wide, ping, pong, slab_ref, lane_ref, outgoing, seen, columns, observed, sums_out, sums_in,
-    uth, utl, uh, ul, cross, result, returned, ready,
-    small_sem, load_sem, halo_send, halo_recv, obs_send, obs_recv, col_send, col_recv,
+    uth, utl, uh, ul, result, returned, ready,
+    small_sem, load_sem, halo_send, halo_recv, obs_send, obs_recv, early_send, early_recv, col_send, col_recv,
     sum_send, sum_recv, back_send, back_recv, out_sem,
 ):
     me = lax.axis_index("mem")
@@ -148,14 +147,24 @@
             device_id_type=MESH,
         )
 
-    def col_copy(n, c, chunks):
-        count = chunks * CHUNK
+    def early_copy(n, c):
         first = pl.multiple_of(c * CHUNK, CHUNK)
         return pltpu.make_async_remote_copy(
-            src_ref=outgoing.at[peer(n), pl.ds(first, count), :],
-            dst_ref=columns.at[pl.ds(BACK[n] * OWN + first, count), :],
-            send_sem=col_send.at[n],
-            recv_sem=col_recv.at[BACK[n]],
+            src_ref=outgoing.at[:, peer(n), pl.ds(first, CHUNK), :],
+            dst_ref=columns.at[:, pl.ds(BACK[n] * OWN + first, CHUNK), :],
+            send_sem=early_send.at[n],
+            recv_sem=early_recv.at[BACK[n]],
+            device_id={"mem": peer(n)},
+            device_id_type=MESH,
+        )
+
+    def col_copy(n, f):
+        count = OWN - EARLY * CHUNK
+        return pltpu.make_async_remote_copy(
+            src_ref=outgoing.at[f, peer(n), pl.ds(EARLY * CHUNK, count), :],
+            dst_ref=columns.at[f, pl.ds(BACK[n] * OWN + EARLY * CHUNK, count), :],
+            send_sem=col_send.at[f, n],
+            recv_sem=col_recv.at[f, BACK[n]],
             device_id={"mem": peer(n)},
             device_id_type=MESH,
         )
@@ -170,12 +179,12 @@
             device_id_type=MESH,
         )
 
-    def back_copy(n):
-        return pltpu.make_async_remote_copy(
-            src_ref=result.at[block(n), :],
-            dst_ref=returned.at[me],
-            send_sem=back_send.at[n],
-            recv_sem=back_recv.at[me],
+    def back_copy(n, f):
+        return pltpu.make_async_remote_copy(
+            src_ref=result.at[f, block(n), :],
+            dst_ref=returned.at[f, me],
+            send_sem=back_send.at[f, n],
+            recv_sem=back_recv.at[f, me],
             device_id={"mem": peer(n)},
             device_id_type=MESH,
         )
@@ -257,7 +266,7 @@
             for f in range(3):
                 for half in range(2):
                     values = new[f][:, half * LANES : (half + 1) * LANES]
-                    outgoing[2 * i + half, part, f * LANES : (f + 1) * LANES] = values
+                    outgoing[f, 2 * i + half, part, :] = values
                     slab = f * (2 * ROWS) + 2 * i + half
                     for g in range(2):
                         lanes = slice(g * LANES, (g + 1) * LANES)
@@ -284,16 +293,16 @@
         @pl.when(c < EARLY)
         def _():
             for n in OTHERS:
-                col_copy(n, c, 1).start()
+                early_copy(n, c).start()
 
         return carry
 
     lax.fori_loop(0, CHUNKS, forecast, 0)
-    for n in OTHERS:
-        col_copy(n, EARLY, CHUNKS - EARLY).start()
+    for f in range(3):
+        for n in OTHERS:
+            col_copy(n, f).start()
     observed[block(SELF), :] = seen[...]
-    columns[block(SELF), :] = outgoing[me]
-    near = jnp.sum(outgoing[me], axis=0, keepdims=True) * (1.0 / OWN)
+    columns[:, block(SELF), :] = outgoing[:, me]
 
     for n in OTHERS:
         wait_for(observed.at[block(n), :], obs_recv.at[n])
@@ -302,12 +311,8 @@
     misfit = goal - obs_mean
     square = jnp.zeros((1, OBS), F32)
     for b in range(SIDE):
-        rows = slice(b * GROUP, (b + 1) * GROUP)
-        centred = observed[rows, :] - obs_mean
+        centred = observed[b * GROUP : (b + 1) * GROUP, :] - obs_mean
         square = square + jnp.sum(centred * centred, axis=0, keepdims=True)
-        scaled = centred * weight
-        uh[rows, :], ul[rows, :] = split(scaled)
-        uth[b], utl[b] = split(scaled.T)
     misfit_sum = total(misfit * misfit)
     spread_sum = total(square * (1.0 / (MEMBERS - 1)) + error)
     upper = lax.broadcasted_iota(jnp.int32, (8, LANES), 0) < 4
@@ -318,7 +323,12 @@
     inner = jnp.zeros((OBS, OBS), F32)
     for b in range(SIDE):
         rows = slice(b * GROUP, (b + 1) * GROUP)
-        inner = inner + dot_split(uth[b], utl[b], uh[rows, :], ul[rows, :])
+        scaled = (observed[rows, :] - obs_mean) * weight
+        u_split = split(scaled)
+        uh[rows, :], ul[rows, :] = u_split
+        ut_split = split(scaled.T)
+        uth[b], utl[b] = ut_split
+        inner = inner + dot_split(*ut_split, *u_split)
     norm = jnp.sqrt(total(inner * inner))
     for k in range(1, N_TILE):
         src = lax.rem(tile + k, N_TILE)
@@ -336,71 +346,79 @@
     ).astype(F32)
     lifted = (scale * gain) * inner
     a = lifted - eye
-    a2 = matmul(a, a)
-    a3 = matmul(a2, a)
-    r = (
+    a_split = split(a)
+    a2 = dot_split(*a_split, *a_split)
+    a3 = dot_split(*split(a2), *a_split)
+    r_split = split(
         c[1] * eye
         + (2.0 * c[2]) * (a - eye)
         + c[3] * (4.0 * (a2 - a) + eye)
         + (8.0 * c[4]) * (a3 - a2)
     )
     lifted_split = split(lifted)
-    r_split = split(r)
-    h = jnp.broadcast_to(misfit * weight, (8, OBS))
-    for _ in range(2):
-        h = p0 * h + dot_split(*split(dot_split(*split(h), *r_split)), *lifted_split)
-    h_split = split(gain * h)
-
-    column_sum = jnp.zeros((1, COLS), F32)
-    for g in ARRIVAL:
-        for n in range(g * SIDE, (g + 1) * SIDE):
-            if n != SELF:
-                wait_for(columns.at[block(n), :], col_recv.at[n])
-        group = columns[g * GROUP : (g + 1) * GROUP, :]
-        column_sum = column_sum + jnp.sum(group, axis=0, keepdims=True)
-        part = dot_split(uth[g], utl[g], *split(group - near))
-        cross[...] = part if g == ARRIVAL[0] else cross[...] + part
-    centre = column_sum * (1.0 / MEMBERS)
-    cross_split = split(cross[...])
-    moved_split = split((root * scale * gain) * dot_split(*r_split, *cross_split))
-    base = centre + dot_split(*h_split, *cross_split)[0:1, :]
+
     keep = root * p0
-    for g in range(SIDE):
-        rows = slice(g * GROUP, (g + 1) * GROUP)
-        shift = dot_split(uh[rows, :], ul[rows, :], *moved_split)
-        result[rows, :] = base + (keep * (columns[rows, :] - centre) + shift)
-        for n in range(g * SIDE, (g + 1) * SIDE):
-            if n != SELF:
-                back_copy(n).start()
-    returned[me] = result[block(SELF), :]
+    for f in range(3):
+        near = jnp.sum(outgoing[f, me], axis=0, keepdims=True) * (1.0 / OWN)
+        column_sum = jnp.zeros((1, LANES), F32)
+        cross = jnp.zeros((OBS, LANES), F32)
+        for g in ARRIVAL:
+            for n in range(g * SIDE, (g + 1) * SIDE):
+                if n != SELF:
+                    if f == 0:
+                        wait_for(columns.at[:, 0 : EARLY * CHUNK, :], early_recv.at[n])
+                    wait_for(columns.at[f, EARLY * CHUNK : OWN, :], col_recv.at[f, n])
+            group = columns[f, g * GROUP : (g + 1) * GROUP, :]
+            column_sum = column_sum + jnp.sum(group, axis=0, keepdims=True)
+            cross = cross + dot_split(uth[g], utl[g], *split(group - near))
+            if f == 0 and g == ARRIVAL[0]:
+                h = jnp.broadcast_to(misfit * weight, (8, OBS))
+                for _ in range(2):
+                    h = p0 * h + dot_split(*split(dot_split(*split(h), *r_split)), *lifted_split)
+                h_split = split(gain * h)
+        centre = column_sum * (1.0 / MEMBERS)
+        cross_split = split(cross)
+        moved_split = split((root * scale * gain) * dot_split(*r_split, *cross_split))
+        base = centre + dot_split(*h_split, *cross_split)[0:1, :]
+        for g in range(SIDE):
+            rows = slice(g * GROUP, (g + 1) * GROUP)
+            shift = dot_split(uh[rows, :], ul[rows, :], *moved_split)
+            result[f, rows, :] = base + (keep * (columns[f, rows, :] - centre) + shift)
+            for n in range(g * SIDE, (g + 1) * SIDE):
+                if n != SELF:
+                    back_copy(n, f).start()
+        returned[f, me] = result[f, block(SELF), :]
 
     finals = []
-    for half in range(2):
-        for i in range(ROWS):
-            src = 2 * i + half
-
-            @pl.when(src != me)
-            def _():
-                wait_for(returned.at[src], back_recv.at[src])
-
-            for m in range(0, OWN, 8):
-                for f in range(3):
+    for f in range(3):
+        for half in range(2):
+            for i in range(ROWS):
+                src = 2 * i + half
+
+                @pl.when(src != me)
+                def _():
+                    wait_for(returned.at[f, src], back_recv.at[f, src])
+
+                for m in range(0, OWN, 8):
                     ready[half, pl.ds(m * LINES + f * ROWS + i, 8, stride=LINES), :] = returned[
-                        src, m : m + 8, f * LANES : (f + 1) * LANES
+                        f, src, m : m + 8, :
                     ]
-        finals.append(
-            pltpu.make_async_copy(
-                ready.at[half], out.at[:, half * LANES : (half + 1) * LANES], out_sem.at[half]
-            )
-        )
-        finals[-1].start()
+            if f == 2:
+                finals.append(
+                    pltpu.make_async_copy(
+                        ready.at[half], out.at[:, half * LANES : (half + 1) * LANES], out_sem.at[half]
+                    )
+                )
+                finals[-1].start()
     for c in range(CHUNKS):
         halo_copy(c, 0).wait_send()
         halo_copy(c, 1).wait_send()
     for n in OTHERS:
         wait_for(seen, obs_send.at[n])
-        wait_for(outgoing.at[0], col_send.at[n])
-        back_copy(n).wait_send()
+        wait_for(outgoing.at[:, 0, 0 : EARLY * CHUNK, :], early_send.at[n])
+        for f in range(3):
+            col_copy(n, f).wait_send()
+            back_copy(n, f).wait_send()
     for k in range(1, N_TILE):
         sum_copy(k, lax.rem(tile + k, N_TILE)).wait_send()
     for copy in finals:
@@ -427,9 +445,9 @@
             pltpu.VMEM((3, ROWS + 4, CHUNK, LONS), F32),
             pltpu.VMEM((8, OBS), jnp.int32),
             pltpu.VMEM((8, OBS), jnp.int32),
-            pltpu.VMEM((N_MEM, OWN, COLS), F32),
+            pltpu.VMEM((3, N_MEM, OWN, LANES), F32),
             pltpu.VMEM((OWN, OBS), F32),
-            pltpu.VMEM((MEMBERS, COLS), F32),
+            pltpu.VMEM((3, MEMBERS, LANES), F32),
             pltpu.VMEM((MEMBERS, OBS), F32),
             pltpu.VMEM((8, LANES), F32),
             pltpu.VMEM((N_TILE, 8, LANES), F32),
@@ -437,9 +455,8 @@
             pltpu.VMEM((SIDE, OBS, GROUP), BF16),
             pltpu.VMEM((MEMBERS, OBS), BF16),
             pltpu.VMEM((MEMBERS, OBS), BF16),
-            pltpu.VMEM((OBS, COLS), F32),
-            pltpu.VMEM((MEMBERS, COLS), F32),
-            pltpu.VMEM((N_MEM, OWN, COLS), F32),
+            pltpu.VMEM((3, MEMBERS, LANES), F32),
+            pltpu.VMEM((3, N_MEM, OWN, LANES), F32),
             pltpu.VMEM((2, OWN * LINES, LANES), F32),
             dma((4,)),
             dma((CHUNKS, 2)),
@@ -449,10 +466,12 @@
             dma((N_MEM,)),
             dma((N_MEM,)),
             dma((N_MEM,)),
+            dma((3, N_MEM)),
+            dma((3, N_MEM)),
             dma((N_TILE,)),
             dma((N_TILE,)),
-            dma((N_MEM,)),
-            dma((N_MEM,)),
+            dma((3, N_MEM)),
+            dma((3, N_MEM)),
             dma((2,)),
         ],
         compiler_params=pltpu.CompilerParams(

time: 73.6 us -> 70.7 us (0.961)
  Pallas kernels: 70.8 us -> 67.9 us
    pallas_call x1, Pallas kernels: 70.8 us -> 67.9 us  [on_device(): pl.pallas_call(kernel, name='analysis', out_shape=jax.ShapeDtypeStruct((O...]
where the time goes in v2:
time: 70.7 us; the launch traced here: 70.6 us
  Pallas kernels  67.9 us (96%)
  local copies, waits for them, and re-layouts  2.65 us (4%)
    pallas_call x1, Pallas kernels, on_device(): pl.pallas_call(kernel, name='analysis', out_shape=jax.ShapeDtypeStruct((O...  67.9 us
    unnamed x1, local copies, waits for them, and re-layouts  2.65 us

profile of v2, /device:TPU:1, one launch (start us, length us, event | category | flops | bytes accessed | tf_op | source)
XLA Modules:
  0.0 70.6 jit_solution(10533761460337577770)
XLA Ops:
  0.0 67.9 %analysis.1 = f32[1536,256]{1,0:T(8,128)} custom-call(f32[1536,256]{1,0:T(8,128)} %bitcast.3, s32[16,256]{1,0:T(8,128)} %cells_in.1, s32[16]{0:T(128)} %region_in.1, f32[16,256]{1,0:T(8,128)} %goals_in.1, f32[16,256]{1,0:T(8,128)} %errors_in.1), custom_call_target="tpu_custom_call" | custom-call | tf_op jit(solution)/shard_map/analysis/pallas_call | solution.py:431
  67.9 2.7 %copy.7 = f32[64,3,8,256]{3,2,1,0:T(8,128)} copy(f32[64,3,8,256]{3,2,1,0:T(8,128)} %bitcast.2) | data formatting | bytes 3145728

commit v3 on v2

--- a/solution.py
+++ b/solution.py
@@ -215,6 +215,23 @@
         to = lax.rem(tile + k, N_TILE)
         pl.semaphore_signal(barrier, inc=1, device_id={"tile": to}, device_id_type=MESH)
 
+    for c in range(CHUNKS):
+        for copy in load_copy(c):
+            copy.wait()
+        for m in range(c * CHUNK, (c + 1) * CHUNK, 8):
+            for f in range(3):
+                for i in range(ROWS):
+                    first = m * LINES + f * ROWS + i
+                    for half in range(2):
+                        lanes = slice(half * LANES, (half + 1) * LANES)
+                        wide[f, STEPS + i, m : m + 8, lanes] = raw[
+                            half, pl.ds(first, 8, stride=LINES), :
+                        ]
+        if c == 0:
+            pl.semaphore_wait(barrier, N_MEM + N_TILE - 2)
+        halo_copy(c, 0).start()
+        halo_copy(c, 1).start()
+
     for copy in small:
         copy.wait()
     cells = jnp.zeros((1, OBS), jnp.int32)
@@ -228,22 +245,6 @@
     cells = jnp.broadcast_to(cells, (8, OBS))
     slab_ref[...] = lax.shift_right_logical(cells, 7)
     lane_ref[...] = lax.bitwise_and(cells, LANES - 1)
-    for c in range(CHUNKS):
-        for copy in load_copy(c):
-            copy.wait()
-        for m in range(c * CHUNK, (c + 1) * CHUNK, 8):
-            for f in range(3):
-                for i in range(ROWS):
-                    first = m * LINES + f * ROWS + i
-                    for half in range(2):
-                        lanes = slice(half * LANES, (half + 1) * LANES)
-                        wide[f, STEPS + i, m : m + 8, lanes] = raw[
-                            half, pl.ds(first, 8, stride=LINES), :
-                        ]
-    pl.semaphore_wait(barrier, N_MEM + N_TILE - 2)
-    for c in range(CHUNKS):
-        halo_copy(c, 0).start()
-        halo_copy(c, 1).start()
 
     def forecast(c, carry):
         part = members(c)
@@ -260,33 +261,34 @@
         step(ROWS + 4, lambda f, i: ping[f, i], pong)
         step(ROWS + 2, lambda f, i: pong[f, i], ping)
 
-        found = [jnp.zeros((8, LANES), F32)] * (2 * (CHUNK // 8))
         for i in range(ROWS):
             new = advanced(lambda f, k: ping[f, i + k])
             for f in range(3):
                 for half in range(2):
-                    values = new[f][:, half * LANES : (half + 1) * LANES]
-                    outgoing[f, 2 * i + half, part, :] = values
-                    slab = f * (2 * ROWS) + 2 * i + half
+                    lanes = slice(half * LANES, (half + 1) * LANES)
+                    outgoing[f, 2 * i + half, part, :] = new[f][:, lanes]
+
+        @pl.when(lax.rem(c, 2) == 1)
+        def _():
+            pair = pl.ds(pl.multiple_of((c - 1) * CHUNK, 2 * CHUNK), 2 * CHUNK)
+            found = [[jnp.zeros((8, LANES), F32)] * 2 for _ in range(2)]
+            for f in range(3):
+                for j in range(2 * ROWS):
+                    values = outgoing[f, j, pair, :]
                     for g in range(2):
                         lanes = slice(g * LANES, (g + 1) * LANES)
-                        here = slab_ref[:, lanes] == slab
-                        for s in range(CHUNK // 8):
-                            n = g * (CHUNK // 8) + s
+                        here = slab_ref[:, lanes] == f * (2 * ROWS) + j
+                        for s in range(2):
                             taken = jnp.take_along_axis(
                                 values[s * 8 : s * 8 + 8],
                                 lane_ref[:, lanes],
                                 axis=1,
                                 mode="promise_in_bounds",
                             )
-                            found[n] = jnp.where(here, taken, found[n])
-        for g in range(2):
-            for s in range(CHUNK // 8):
-                at = pl.multiple_of(c * CHUNK + s * 8, 8)
-                seen[pl.ds(at, 8), g * LANES : (g + 1) * LANES] = found[g * (CHUNK // 8) + s]
-
-        @pl.when(lax.rem(c, 2) == 1)
-        def _():
+                            found[g][s] = jnp.where(here, taken, found[g][s])
+            for g in range(2):
+                lanes = slice(g * LANES, (g + 1) * LANES)
+                seen[pair, lanes] = jnp.concatenate(found[g], axis=0)
             for n in OTHERS:
                 obs_copy(n, c - 1, 2).start()
 

time: 70.7 us -> 70.1 us (level)
  no operation moved by 1% of the time
where the time goes in v3:
time: 70.1 us; the launch traced here: 70 us
  Pallas kernels  67.3 us (96%)
  local copies, waits for them, and re-layouts  2.65 us (4%)
    pallas_call x1, Pallas kernels, on_device(): pl.pallas_call(kernel, name='analysis', out_shape=jax.ShapeDtypeStruct((O...  67.3 us
    unnamed x1, local copies, waits for them, and re-layouts  2.65 us

profile of v3, /device:TPU:1, one launch (start us, length us, event | category | flops | bytes accessed | tf_op | source)
XLA Modules:
  0.0 70.0 jit_solution(8035349124669008483)
XLA Ops:
  0.0 67.3 %analysis.1 = f32[1536,256]{1,0:T(8,128)} custom-call(f32[1536,256]{1,0:T(8,128)} %bitcast.3, s32[16,256]{1,0:T(8,128)} %cells_in.1, s32[16]{0:T(128)} %region_in.1, f32[16,256]{1,0:T(8,128)} %goals_in.1, f32[16,256]{1,0:T(8,128)} %errors_in.1), custom_call_target="tpu_custom_call" | custom-call | tf_op jit(solution)/shard_map/analysis/pallas_call | solution.py:433
  67.3 2.7 %copy.7 = f32[64,3,8,256]{3,2,1,0:T(8,128)} copy(f32[64,3,8,256]{3,2,1,0:T(8,128)} %bitcast.2) | data formatting | bytes 3145728

commit v4 on v3

--- a/solution.py
+++ b/solution.py
@@ -30,6 +30,9 @@
 PARTNERS = [(dy, (dy + k) % SIDE) for k in (2, 1, 3, 0) for dy in (2, 1, 3, 0)]
 BACK = [PARTNERS.index((-dy % SIDE, -dx % SIDE)) for dy, dx in PARTNERS]
 OTHERS = range(N_MEM - 1)
+ALTERNATING = [(0, 1), (1, 0), (0, 3), (3, 0), (0, 2), (2, 0), (1, 1), (3, 3)]
+ALTERNATING += [(3, 1), (1, 3), (1, 2), (2, 1), (3, 2), (2, 3), (2, 2)]
+SENDS = [PARTNERS.index(offset) for offset in ALTERNATING]
 SELF = N_MEM - 1
 ARRIVAL = (0, 2, 1, 3)
 EARLY = 2
@@ -289,19 +292,19 @@
             for g in range(2):
                 lanes = slice(g * LANES, (g + 1) * LANES)
                 seen[pair, lanes] = jnp.concatenate(found[g], axis=0)
-            for n in OTHERS:
+            for n in SENDS:
                 obs_copy(n, c - 1, 2).start()
 
         @pl.when(c < EARLY)
         def _():
-            for n in OTHERS:
+            for n in SENDS:
                 early_copy(n, c).start()
 
         return carry
 
     lax.fori_loop(0, CHUNKS, forecast, 0)
     for f in range(3):
-        for n in OTHERS:
+        for n in SENDS:
             col_copy(n, f).start()
     observed[block(SELF), :] = seen[...]
     columns[:, block(SELF), :] = outgoing[:, me]

time: 70.1 us -> 70.3 us (level)
  no operation moved by 1% of the time
where the time goes in v4:
time: 70.3 us; the launch traced here: 70.2 us
  Pallas kernels  67.5 us (96%)
  local copies, waits for them, and re-layouts  2.65 us (4%)
    pallas_call x1, Pallas kernels, on_device(): pl.pallas_call(kernel, name='analysis', out_shape=jax.ShapeDtypeStruct((O...  67.5 us
    unnamed x1, local copies, waits for them, and re-layouts  2.65 us

profile of v4, /device:TPU:1, one launch (start us, length us, event | category | flops | bytes accessed | tf_op | source)
XLA Modules:
  0.0 70.2 jit_solution(5043264795832027179)
XLA Ops:
  0.0 67.5 %analysis.1 = f32[1536,256]{1,0:T(8,128)} custom-call(f32[1536,256]{1,0:T(8,128)} %bitcast.3, s32[16,256]{1,0:T(8,128)} %cells_in.1, s32[16]{0:T(128)} %region_in.1, f32[16,256]{1,0:T(8,128)} %goals_in.1, f32[16,256]{1,0:T(8,128)} %errors_in.1), custom_call_target="tpu_custom_call" | custom-call | tf_op jit(solution)/shard_map/analysis/pallas_call | solution.py:436
  67.5 2.7 %copy.7 = f32[64,3,8,256]{3,2,1,0:T(8,128)} copy(f32[64,3,8,256]{3,2,1,0:T(8,128)} %bitcast.2) | data formatting | bytes 3145728
